TPU v7x, 32 devices: a whole 2x2x4 slice. The times are simulated.
32 devices in a mesh: dp: 8 (over z, x), ctx: 4 (over y, core).
Axes of the slice: x: 2, y: 2, z: 4, core: 2. Of those that a mesh axis runs over, the one named last changes fastest.
Arguments:
- tokens: bfloat16 [4096, 1024], P(('dp', 'ctx')), may hold values from -6 to 6
- cotangent: bfloat16 [4096, 1024], P(('dp', 'ctx')), may hold values from -6 to 6
- segment_ids: int32 [8, 512], P('dp'), may hold values from 0 to 3, never falling along the last dimension, each value on 1 to 256 neighbouring positions
- tract_order: int32 [8, 8], P('dp'), may hold values from 0 to 7, each once within a row
- qkv_weight: bfloat16 [1024, 3072], P(('dp', 'ctx')), may hold values from -0.1875 to 0.1875
- out_weight: bfloat16 [1024, 1024], P(('dp', 'ctx')), may hold values from -2 to 2
- up_weight: bfloat16 [1024, 4096], P(('dp', 'ctx')), may hold values from -0.1875 to 0.1875
- down_weight: bfloat16 [4096, 1024], P(('dp', 'ctx')), may hold values from -0.09375 to 0.09375
- norm_gain: bfloat16 [2, 1024], P(None, ('dp', 'ctx')), may hold values from 0.5 to 1.5
- norm_shift: bfloat16 [2, 1024], P(None, ('dp', 'ctx')), may hold values from -4 to 4
- proj_bias: bfloat16 [4, 1024], P(None, ('dp', 'ctx')), may hold values from -6 to 6
- up_bias: bfloat16 [4096], P(('dp', 'ctx')), may hold values from -6 to 6
Outputs:
- block_out: float32 [4096, 1024], P(('dp', 'ctx'))
- input_grad: float32 [4096, 1024], P(('dp', 'ctx'))
- qkv_weight_grad: float32 [1024, 3072], P(('dp', 'ctx'))
- out_weight_grad: float32 [1024, 1024], P(('dp', 'ctx'))
- up_weight_grad: float32 [1024, 4096], P(('dp', 'ctx'))
- down_weight_grad: float32 [4096, 1024], P(('dp', 'ctx'))
- norm_gain_grad: float32 [2, 1024], P(None, ('dp', 'ctx'))
- norm_shift_grad: float32 [2, 1024], P(None, ('dp', 'ctx'))
- proj_bias_grad: float32 [4, 1024], P(None, ('dp', 'ctx'))
- up_bias_grad: float32 [4096], P(('dp', 'ctx'))
Inputs may be any that keep to these rules, and one draw needn't show every extreme that they name: `segment_ids`: along each row the ids never fall; one document covers at most 256 positions of a row. `tract_order`: each row is a permutation: every place 0 to 7 is named once.
All inputs are finite; a program needn't handle non-finite values.
Results may differ from a plain program's by a relative error of at most 0.011.
Values may be sent and summed in bfloat16 or wider, within the bound.
A program may use at most 256 MiB of HBM per device.

v0:
```python
import jax
import jax.numpy as jnp
from jax import lax
from jax.sharding import PartitionSpec as P

HEADS = 16
HEAD_DIM = 64


EPSILON = 1e-05
GELU_COEF = 0.7978845608028654


def gelu_parts(inputs):
    cubed_part = inputs * inputs * inputs
    tanh_part = jnp.tanh(GELU_COEF * (inputs + 0.044715 * cubed_part))
    values = 0.5 * inputs * (1.0 + tanh_part)
    slopes = 0.5 * (1.0 + tanh_part) + 0.5 * inputs * (1.0 - tanh_part * tanh_part) * GELU_COEF * (
        1.0 + 3.0 * 0.044715 * inputs * inputs
    )
    return (values, slopes)


def norm_parts(values):
    centred = values - jnp.mean(values, axis=-1, keepdims=True)
    inverse = lax.rsqrt(jnp.mean(centred * centred, axis=-1, keepdims=True) + EPSILON)
    return (centred * inverse, inverse)


def norm_back(grads, normed, inverse, gain_row):
    scaled = grads * gain_row
    return inverse * (
        scaled
        - jnp.mean(scaled, axis=-1, keepdims=True)
        - normed * jnp.mean(scaled * normed, axis=-1, keepdims=True)
    )


def outer_sum(former, latter):
    return lax.dot_general(
        former, latter, (((0,), (0,)), ((), ())), preferred_element_type=jnp.float32
    )


def back_product(former, latter):
    return lax.dot_general(
        former, latter, (((1,), (1,)), ((), ())), preferred_element_type=jnp.float32
    )


def shards(
    tokens,
    cotangent,
    segment_ids,
    tract_order,
    qkv_weight,
    out_weight,
    up_weight,
    down_weight,
    norm_gain,
    norm_shift,
    proj_bias,
    up_bias,
):
    row_count = tokens.shape[0]
    block_rows = row_count // 2
    feat_width = tokens.shape[1]
    attn_scale = HEAD_DIM ** (-0.5)
    gathered = (
        lax.all_gather(qkv_weight, ("dp", "ctx"), axis=0, tiled=True),
        lax.all_gather(out_weight, ("dp", "ctx"), axis=0, tiled=True),
        lax.all_gather(up_weight, ("dp", "ctx"), axis=0, tiled=True),
        lax.all_gather(down_weight, ("dp", "ctx"), axis=0, tiled=True),
        lax.all_gather(norm_gain, ("dp", "ctx"), axis=1, tiled=True),
        lax.all_gather(norm_shift, ("dp", "ctx"), axis=1, tiled=True),
        lax.all_gather(proj_bias, ("dp", "ctx"), axis=1, tiled=True),
        lax.all_gather(up_bias, ("dp", "ctx"), axis=0, tiled=True),
    )
    qkv_full, out_full, up_full, down_full, gain_full, shift_full, bias_full, upb_full = gathered
    gains = gain_full.astype(jnp.float32)
    shifts = shift_full.astype(jnp.float32)
    biases = bias_full.astype(jnp.float32)
    up_shift = upb_full.astype(jnp.float32)
    block_ranks = tract_order[0]
    positions = (
        block_ranks[:, None] * block_rows + jnp.arange(block_rows, dtype=jnp.int32)[None, :]
    ).reshape(-1)
    segments = jnp.take(segment_ids[0].reshape(-1, block_rows), block_ranks, axis=0).reshape(-1)
    first_row = lax.axis_index("ctx") * row_count
    local_pos = lax.dynamic_slice_in_dim(positions, first_row, row_count)
    local_seg = lax.dynamic_slice_in_dim(segments, first_row, row_count)

    def allowed_keys():
        return (positions[None, :] <= local_pos[:, None]) & (
            segments[None, :] == local_seg[:, None]
        )

    resid_in = tokens.astype(jnp.float32)
    normed_one, inverse_one = norm_parts(resid_in)
    normed_in = (normed_one * gains[0] + shifts[0]).astype(jnp.bfloat16)
    projected = jnp.dot(normed_in, qkv_full, preferred_element_type=jnp.float32)
    query_rows = (projected[:, :feat_width] + biases[0]).astype(jnp.bfloat16)
    key_rows = projected[:, feat_width : 2 * feat_width].astype(jnp.bfloat16)
    value_rows = (projected[:, 2 * feat_width :] + biases[1]).astype(jnp.bfloat16)
    query_heads = query_rows.reshape(row_count, HEADS, HEAD_DIM)
    key_part = lax.all_gather(key_rows, "ctx", axis=0, tiled=True)
    value_part = lax.all_gather(value_rows, "ctx", axis=0, tiled=True)
    span_rows = key_part.shape[0]
    key_heads = key_part.reshape(span_rows, HEADS, HEAD_DIM)
    value_heads = value_part.reshape(span_rows, HEADS, HEAD_DIM)
    scores = (
        jnp.einsum("qhd,khd->hqk", query_heads, key_heads, preferred_element_type=jnp.float32)
        * attn_scale
    )
    exp_weights = jnp.where(allowed_keys()[None], jnp.exp(scores), 0.0)
    numerator = jnp.einsum(
        "hqk,khd->qhd",
        exp_weights.astype(jnp.bfloat16),
        value_heads,
        preferred_element_type=jnp.float32,
    ).reshape(row_count, feat_width)
    denominator = jnp.sum(exp_weights, axis=-1)
    numerator, denominator = (numerator, denominator)
    attended = (
        (numerator.reshape(row_count, HEADS, HEAD_DIM) / denominator.T[:, :, None])
        .reshape(row_count, feat_width)
        .astype(jnp.bfloat16)
    )
    log_total = jnp.log(denominator)
    resid_mid = (
        resid_in + jnp.dot(attended, out_full, preferred_element_type=jnp.float32) + biases[2]
    )
    normed_two, inverse_two = norm_parts(resid_mid)
    normed_mid = (normed_two * gains[1] + shifts[1]).astype(jnp.bfloat16)
    pre_act = jnp.dot(normed_mid, up_full, preferred_element_type=jnp.float32) + up_shift
    activated, slopes = gelu_parts(pre_act)
    act_rows = activated.astype(jnp.bfloat16)
    block_out = (
        resid_mid + jnp.dot(act_rows, down_full, preferred_element_type=jnp.float32) + biases[3]
    )
    regathered = (
        lax.all_gather(qkv_weight, ("dp", "ctx"), axis=0, tiled=True),
        lax.all_gather(out_weight, ("dp", "ctx"), axis=0, tiled=True),
        lax.all_gather(up_weight, ("dp", "ctx"), axis=0, tiled=True),
        lax.all_gather(down_weight, ("dp", "ctx"), axis=0, tiled=True),
        lax.all_gather(norm_gain, ("dp", "ctx"), axis=1, tiled=True),
        lax.all_gather(norm_shift, ("dp", "ctx"), axis=1, tiled=True),
        lax.all_gather(proj_bias, ("dp", "ctx"), axis=1, tiled=True),
        lax.all_gather(up_bias, ("dp", "ctx"), axis=0, tiled=True),
    )
    qkv_back, out_back, up_back, down_back = (
        regathered[0],
        regathered[1],
        regathered[2],
        regathered[3],
    )
    gains_back = regathered[4].astype(jnp.float32)
    grad_top = cotangent.astype(jnp.float32)
    grad_act = back_product(cotangent, down_back)
    grad_pre = grad_act * slopes
    grad_pre_low = grad_pre.astype(jnp.bfloat16)
    grad_norm_two = back_product(grad_pre_low, up_back)
    grad_mid = grad_top + norm_back(grad_norm_two, normed_two, inverse_two, gains_back[1])
    grad_mid_low = grad_mid.astype(jnp.bfloat16)
    grad_att = back_product(grad_mid_low, out_back).astype(jnp.bfloat16)
    grad_att_heads = grad_att.reshape(row_count, HEADS, HEAD_DIM)
    delta_rows = jnp.sum(
        grad_att_heads.astype(jnp.float32)
        * attended.reshape(row_count, HEADS, HEAD_DIM).astype(jnp.float32),
        axis=-1,
    ).T
    key_part = lax.all_gather(key_rows, "ctx", axis=0, tiled=True)
    value_part = lax.all_gather(value_rows, "ctx", axis=0, tiled=True)
    span_rows = key_part.shape[0]
    key_heads = key_part.reshape(span_rows, HEADS, HEAD_DIM)
    value_heads = value_part.reshape(span_rows, HEADS, HEAD_DIM)
    scores = (
        jnp.einsum("qhd,khd->hqk", query_heads, key_heads, preferred_element_type=jnp.float32)
        * attn_scale
    )
    soft_weights = jnp.where(allowed_keys()[None], jnp.exp(scores - log_total[:, :, None]), 0.0)
    value_grad_part = jnp.einsum(
        "hqk,qhd->khd",
        soft_weights.astype(jnp.bfloat16),
        grad_att_heads,
        preferred_element_type=jnp.float32,
    ).reshape(span_rows, feat_width)
    grad_probs = jnp.einsum(
        "qhd,khd->hqk", grad_att_heads, value_heads, preferred_element_type=jnp.float32
    )
    grad_scores = (soft_weights * (grad_probs - delta_rows[:, :, None])).astype(jnp.bfloat16)
    grad_query = (
        jnp.einsum(
            "hqk,khd->qhd", grad_scores, key_heads, preferred_element_type=jnp.float32
        ).reshape(row_count, feat_width)
        * attn_scale
    )
    key_grad_part = (
        jnp.einsum(
            "hqk,qhd->khd", grad_scores, query_heads, preferred_element_type=jnp.float32
        ).reshape(span_rows, feat_width)
        * attn_scale
    )
    folded = (grad_query, key_grad_part, value_grad_part)
    grad_query = folded[0]
    own_keys, own_values = (
        lax.psum_scatter(
            folded[1].astype(jnp.bfloat16), "ctx", scatter_dimension=0, tiled=True
        ).astype(jnp.float32),
        lax.psum_scatter(
            folded[2].astype(jnp.bfloat16), "ctx", scatter_dimension=0, tiled=True
        ).astype(jnp.float32),
    )
    grad_proj = jnp.concatenate([grad_query, own_keys, own_values], axis=1).astype(jnp.bfloat16)
    grad_norm_one = back_product(grad_proj, qkv_back)
    input_grad = grad_mid + norm_back(grad_norm_one, normed_one, inverse_one, gains_back[0])
    grad_gain = jnp.stack(
        [jnp.sum(grad_norm_one * normed_one, axis=0), jnp.sum(grad_norm_two * normed_two, axis=0)]
    )
    grad_shift = jnp.stack([jnp.sum(grad_norm_one, axis=0), jnp.sum(grad_norm_two, axis=0)])
    grad_bias = jnp.stack(
        [
            jnp.sum(grad_query, axis=0),
            jnp.sum(own_values, axis=0),
            jnp.sum(grad_mid, axis=0),
            jnp.sum(grad_top, axis=0),
        ]
    )
    grad_upb = jnp.sum(grad_pre, axis=0)
    front_owned = lax.psum_scatter(
        jnp.concatenate(
            [
                outer_sum(normed_in, grad_proj),
                outer_sum(attended, grad_mid_low),
                outer_sum(normed_mid, grad_pre_low),
            ],
            axis=1,
        ),
        ("dp", "ctx"),
        scatter_dimension=0,
        tiled=True,
    )
    down_owned = lax.psum_scatter(
        outer_sum(act_rows, cotangent), ("dp", "ctx"), scatter_dimension=0, tiled=True
    )
    small_owned = (
        lax.psum_scatter(grad_gain, ("dp", "ctx"), scatter_dimension=1, tiled=True),
        lax.psum_scatter(grad_shift, ("dp", "ctx"), scatter_dimension=1, tiled=True),
        lax.psum_scatter(grad_bias, ("dp", "ctx"), scatter_dimension=1, tiled=True),
        lax.psum_scatter(grad_upb, ("dp", "ctx"), scatter_dimension=0, tiled=True),
    )
    qkv_grad = front_owned[:, : 3 * feat_width]
    outw_grad = front_owned[:, 3 * feat_width : 4 * feat_width]
    up_grad = front_owned[:, 4 * feat_width :]
    return (
        block_out,
        input_grad,
        qkv_grad,
        outw_grad,
        up_grad,
        down_owned,
        small_owned[0],
        small_owned[1],
        small_owned[2],
        small_owned[3],
    )


def solution(mesh):
    return jax.shard_map(
        shards,
        mesh=mesh,
        in_specs=(
            P(("dp", "ctx"), None),
            P(("dp", "ctx"), None),
            P("dp", None),
            P("dp", None),
            P(("dp", "ctx"), None),
            P(("dp", "ctx"), None),
            P(("dp", "ctx"), None),
            P(("dp", "ctx"), None),
            P(None, ("dp", "ctx")),
            P(None, ("dp", "ctx")),
            P(None, ("dp", "ctx")),
            P(("dp", "ctx")),
        ),
        out_specs=(
            P(("dp", "ctx"), None),
            P(("dp", "ctx"), None),
            P(("dp", "ctx"), None),
            P(("dp", "ctx"), None),
            P(("dp", "ctx"), None),
            P(("dp", "ctx"), None),
            P(None, ("dp", "ctx")),
            P(None, ("dp", "ctx")),
            P(None, ("dp", "ctx")),
            P(("dp", "ctx")),
        ),
        check_vma=False,
    )
```

profile of v0, /device:TPU:0, one launch (start us, length us, event | category | flops | bytes accessed | tf_op | source)
XLA Modules:
  0.0 1404.0 jit_solution(15542381055775052535)
XLA Ops:
  8.0 43.5 %all-gather = bf16[32,32,2]{1,2,0:T(2,128)(2,1)S(1)} all-gather(bf16[1,32,2]{1,2,0:T(2,128)(2,1)} %bitcast.147), channel_id=1, replica_groups=mesh['dp'=8,'ctx'=4] {'dp','ctx'}, dimensions={0}, use_global_device_ids=true | all-gather | bytes 4224 | tf_op jit(solution)/shard_map/all_gather | solution.py:74
  51.5 37.2 %all-gather.1 = bf16[32,32,2]{1,2,0:T(2,128)(2,1)S(1)} all-gather(bf16[1,32,2]{1,2,0:T(2,128)(2,1)} %bitcast.148), channel_id=1, replica_groups=mesh['dp'=8,'ctx'=4] {'dp','ctx'}, dimensions={0}, use_global_device_ids=true | all-gather | bytes 4224 | tf_op jit(solution)/shard_map/all_gather | solution.py:75
  89.9 1.2 fusion.48
  91.1 4.0 fusion.68
  95.9 38.2 %all-gather.2 = bf16[32,32,4]{1,2,0:T(4,128)(2,1)S(1)} all-gather(bf16[1,32,4]{1,2,0:T(4,128)(2,1)S(1)} %bitcast.146), channel_id=1, replica_groups=mesh['dp'=8,'ctx'=4] {'dp','ctx'}, dimensions={0}, use_global_device_ids=true | all-gather | bytes 8448 | tf_op jit(solution)/shard_map/all_gather | solution.py:76
  139.2 36.8 %all-gather.3 = bf16[32,1,128]{2,1,0:T(2,128)(2,1)S(1)} all-gather(bf16[1,1,128]{2,1,0:T(2,128)(2,1)S(1)} %bitcast.149), channel_id=1, replica_groups=mesh['dp'=8,'ctx'=4] {'dp','ctx'}, dimensions={0}, use_global_device_ids=true | all-gather | bytes 8448 | tf_op jit(solution)/shard_map/all_gather | solution.py:77
  176.4 1.6 copy.51
  178.0 3.0 fusion
  181.0 1.5 copy.49
  182.5 3.5 fusion.32
  186.0 21.1 %all-gather.17.cloned.1.call-done = bf16[1024,1024]{1,0:T(8,128)(2,1)} async-done(((bf16[32,1024]{1,0:T(8,128)(2,1)}), bf16[1024,1024]{1,0:T(8,128)(2,1)}) %all-gather.17.cloned.1.call-update) | async-done | bytes 2097168 | tf_op jit(solution)/shard_map/all_gather | solution.py:71
  207.1 2.1 fusion.76
  209.5 76.3 %all-gather.19.cloned.1.call-done = bf16[1024,4096]{1,0:T(8,128)(2,1)} async-done(((bf16[32,4096]{1,0:T(8,128)(2,1)}), bf16[1024,4096]{1,0:T(8,128)(2,1)}) %all-gather.19.cloned.1.call-update) | async-done | bytes 8388624 | tf_op jit(solution)/shard_map/all_gather | solution.py:72
  285.8 4.8 convolution_add_fusion
  290.6 73.7 %all-gather.21.cloned.1.call-done = bf16[4096,1024]{1,0:T(8,128)(2,1)} async-done(((bf16[128,1024]{1,0:T(8,128)(2,1)}), bf16[4096,1024]{1,0:T(8,128)(2,1)}) %all-gather.21.cloned.1.call-update) | async-done | bytes 8388624 | tf_op jit(solution)/shard_map/all_gather | solution.py:73
  364.2 7.0 fusion.77
  371.3 3.0 multiply_reduce_fusion
  374.7 1.5 convolution_convert_fusion
  376.2 1.8 copy.52
  378.0 4.3 fusion.21
  382.3 2.3 copy.57
  386.0 4.2 multiply_convert_fusion
  390.2 1.3 copy-done.3
  391.6 1.4 multiply_convert_fusion.1
  393.0 2.3 copy.55
  395.3 3.5 fusion.72
  398.9 3.7 fusion.57
  402.6 8.2 fusion.51
  410.7 1.8 copy.58
  413.6 21.9 %reduce-scatter.22.cloned.1.call-done = bf16[128,1024]{1,0:T(8,128)(2,1)} async-done(((bf16[512,1024]{1,0:T(8,128)(2,1)}), bf16[128,1024]{1,0:T(8,128)(2,1)}) %reduce-scatter.22.cloned.1.call-update) | async-done | bytes 262160
  435.6 1.8 copy.56
  437.4 7.6 fusion.55
  445.0 5.8 fusion.47
  454.3 22.8 %pad_maximum_fusion = f32[1024,8192]{1,0:T(8,128)} fusion(f32[1024,4096]{1,0:T(8,128)} %fusion.51, f32[1024,1024]{1,0:T(8,128)} %fusion.57, f32[1024,3072]{1,0:T(8,128)} %fusion.55), kind=kLoop, calls=%fused_computation.1 | loop fusion | flops 16777216 | bytes 67108864 | tf_op jit(solution)/shard_map/concatenate | solution.py:231
  477.4 9.0 fusion.70
  486.4 39.5 %all-reduce = f32[4096]{0:T(1024)S(1)} all-reduce(f32[4096]{0:T(1024)S(1)} %get-tuple-element.40), channel_id=9, replica_groups=mesh['dp'=8,'ctx'=4] {'dp','ctx'}, use_global_device_ids=true, to_apply=%region_26.27.clone | all-reduce | flops 4096 | bytes 32768
  526.5 5.7 fusion.28
  533.3 54.8 %reduce-scatter.28.cloned.1.call-done = f32[32,2]{1,0:T(8,128)} async-done(((f32[1024,2]{1,0:T(8,128)}), f32[32,2]{1,0:T(8,128)}) %reduce-scatter.28.cloned.1.call-update) | async-done | bytes 272
  588.1 1.4 copy.62
  589.4 132.3 %reduce-scatter.26.cloned.1.call-done = f32[32,2]{1,0:T(8,128)} async-done(((f32[1024,2]{1,0:T(8,128)}), f32[32,2]{1,0:T(8,128)}) %reduce-scatter.26.cloned.1.call-update) | async-done | bytes 272
  721.8 1.4 copy.60
  723.1 132.6 %reduce-scatter.30.cloned.1.call-done = f32[32,4]{1,0:T(8,128)} async-done(((f32[1024,4]{1,0:T(8,128)}), f32[32,4]{1,0:T(8,128)}) %reduce-scatter.30.cloned.1.call-update) | async-done | bytes 528
  855.7 1.4 copy.64
  857.1 350.9 %reduce-scatter.18.cloned.1.call-done = f32[32,8192]{1,0:T(8,128)} async-done(((f32[1024,8192]{1,0:T(8,128)}), f32[32,8192]{1,0:T(8,128)}) %reduce-scatter.18.cloned.1.call-update) | async-done | bytes 1048592 | tf_op jit(solution)/shard_map/reduce_scatter | solution.py:230
  1208.0 1.6 slice.73
  1209.5 1.8 slice.72
  1211.3 1.9 slice.74
  1213.2 184.3 %reduce-scatter.20.cloned.1.call-done = f32[128,1024]{1,0:T(8,128)} async-done(((f32[4096,1024]{1,0:T(8,128)}), f32[128,1024]{1,0:T(8,128)}) %reduce-scatter.20.cloned.1.call-update) | async-done | bytes 524304 | tf_op jit(solution)/shard_map/reduce_scatter | solution.py:243
  (121 shorter events, 16.8 us)
Async XLA Ops:
  7.2 83.9 %all-gather.11.cloned.1.call-start = ((), (), s32[]{:S(2)}) async-start(), calls=%async_computation.7 | async-start | bytes 6488064 | tf_op jit(solution)/shard_map/all_gather | solution.py:70
  7.9 168.4 %all-gather.15.cloned.1.call-start = ((), (), s32[]{:S(2)}) async-start(), calls=%async_computation.9 | async-start | bytes 1310720 | tf_op jit(solution)/shard_map/all_gather | solution.py:106
  91.1 4.8 copy-start.18
  95.1 42.3 %copy-start.17 = (s32[1,512]{1,0:T(1,128)S(1)}, s32[1,512]{1,0:T(1,128)}, u32[]{:S(2)}) copy-start(s32[1,512]{1,0:T(1,128)} %param.14) | copy-start | bytes 6148
  95.1 43.0 %copy-start.20 = (s32[1,8]{1,0:T(1,128)S(1)}, s32[1,8]{1,0:T(1,128)}, u32[]{:S(2)}) copy-start(s32[1,8]{1,0:T(1,128)} %param.15) | copy-start | bytes 100
  95.1 44.1 %copy-start.19 = (bf16[128]{0:T(256)(128)(2,1)S(1)}, bf16[128]{0:T(256)(128)(2,1)}, u32[]{:S(2)}) copy-start(bf16[128]{0:T(256)(128)(2,1)} %param.23) | copy-start | bytes 772
  95.9 85.1 %all-gather.13.cloned.1.call-start = ((), (), s32[]{:S(2)}) async-start(), calls=%async_computation.8 | async-start | bytes 1310720 | tf_op jit(solution)/shard_map/all_gather | solution.py:107
  135.1 72.0 %all-gather.17.cloned.1.call-start = ((), (), s32[]{:S(2)}) async-start(), calls=%async_computation.10 | async-start | bytes 2162688 | tf_op jit(solution)/shard_map/all_gather | solution.py:71
  135.6 150.1 %all-gather.19.cloned.1.call-start = ((), (), s32[]{:S(2)}) async-start(), calls=%async_computation.11 | async-start | bytes 8650752 | tf_op jit(solution)/shard_map/all_gather | solution.py:72
  136.2 228.0 %all-gather.21.cloned.1.call-start = ((), (), s32[]{:S(2)}) async-start(), calls=%async_computation.12 | async-start | bytes 8650752 | tf_op jit(solution)/shard_map/all_gather | solution.py:73
  136.8 273.9 %reduce-scatter.24.cloned.1.call-start = ((), (), s32[]{:S(2)}) async-start(), calls=%async_computation.16 | async-start | bytes 1310720
  176.3 4.6 copy-start.14
  177.9 3.0 copy-start.6
  182.5 3.5 copy-start.12
  182.5 24.6 %copy-start.1 = (bf16[128,1024]{1,0:T(8,128)(2,1)S(1)}, bf16[128,1024]{1,0:T(8,128)(2,1)}, u32[]{:S(2)}) copy-start(bf16[128,1024]{1,0:T(8,128)(2,1)} %param.12) | copy-start | bytes 786436
  186.0 99.8 %copy-start.8 = (bf16[128,16,64]{0,2,1:T(8,128)(2,1)}, bf16[128,16,64]{0,2,1:T(8,128)(2,1)S(1)}, u32[]{:S(2)}) copy-start(bf16[128,16,64]{0,2,1:T(8,128)(2,1)S(1)} %fusion.32) | copy-start | bytes 786436
  285.8 78.4 %copy-start.9 = (bf16[128,1024]{1,0:T(8,128)(2,1)S(1)}, bf16[128,1024]{1,0:T(8,128)(2,1)}, u32[]{:S(2)}) copy-start(bf16[128,1024]{1,0:T(8,128)(2,1)} %param.13) | copy-start | bytes 786436
  364.2 7.1 copy-start
  371.3 3.1 copy-start.4
  371.3 3.1 copy-start.10
  371.3 3.4 copy-start.2
  384.6 50.9 %reduce-scatter.22.cloned.1.call-start = ((), (), s32[]{:S(2)}) async-start(), calls=%async_computation.15 | async-start | bytes 1310720
  386.0 5.5 copy-start.15
  390.2 1.4 copy-start.3
  395.3 192.8 %reduce-scatter.28.cloned.1.call-start = ((), (), s32[]{:S(2)}) async-start(), calls=%async_computation.18 | async-start | bytes 540672
  398.9 3.7 copy-start.5
  437.4 7.6 copy-start.7
  437.4 7.6 copy-start.11
  437.4 7.6 copy-start.13
  452.0 269.8 %reduce-scatter.26.cloned.1.call-start = ((), (), s32[]{:S(2)}) async-start(), calls=%async_computation.17 | async-start | bytes 540672
  453.1 402.6 %reduce-scatter.30.cloned.1.call-start = ((), (), s32[]{:S(2)}) async-start(), calls=%async_computation.19 | async-start | bytes 540672
  454.2 753.7 %reduce-scatter.18.cloned.1.call-start = ((), (), s32[]{:S(2)}) async-start(), calls=%async_computation.13 | async-start | bytes 34603008 | tf_op jit(solution)/shard_map/reduce_scatter | solution.py:230
  477.1 920.4 %reduce-scatter.20.cloned.1.call-start = ((), (), s32[]{:S(2)}) async-start(), calls=%async_computation.14 | async-start | bytes 17301504 | tf_op jit(solution)/shard_map/reduce_scatter | solution.py:243
  526.5 5.8 copy-start.16
Sparse Core Ops, SparseCore 0:
  10.9 72.0 all-gather.10
  96.0 14.2 all-gather.14
  135.2 12.8 all-gather.12
  150.8 56.2 all-gather.16
  209.8 75.9 all-gather.18
  288.5 75.6 all-gather.20
  384.8 23.4 reduce-scatter.23
  410.7 24.7 reduce-scatter.21
  452.1 135.9 reduce-scatter.27
  590.2 131.5 reduce-scatter.25
  724.0 131.6 reduce-scatter.29
  857.9 350.0 reduce-scatter.17
  1210.8 186.6 reduce-scatter.19
where the time goes:
time: 1410 us; the launch traced here: 1400 us
  waiting for transfers between devices  1050 us (74%)
  blocking collectives  195 us (14%)
  matrix products  82.4 us (6%)
  other arithmetic  30.6 us (2%)
  local copies, waits for them, and re-layouts  30.2 us (2%)
  between operations  14.3 us (1%)
    reduce_scatter x1, waiting for transfers between devices, shards(): lax.psum_scatter(jnp.concatenate([outer_sum(normed_in, grad_proj), outer_...  351 us
    unnamed x18, waiting for transfers between devices  344 us
    reduce_scatter x1, waiting for transfers between devices, shards(): lax.psum_scatter(outer_sum(act_rows, cotangent), ('dp', 'ctx'), scatter_d...  184 us
    all_gather x1, waiting for transfers between devices, shards(): lax.all_gather(up_weight, ('dp', 'ctx'), axis=0, tiled=True)  76.3 us
    all_gather x1, waiting for transfers between devices, shards(): lax.all_gather(down_weight, ('dp', 'ctx'), axis=0, tiled=True)  73.7 us
    all_gather x1, blocking collectives, shards(): lax.all_gather(norm_gain, ('dp', 'ctx'), axis=1, tiled=True)  43.5 us
    unnamed x1, blocking collectives  39.5 us
    all_gather x1, blocking collectives, shards(): lax.all_gather(proj_bias, ('dp', 'ctx'), axis=1, tiled=True)  38.2 us
  transfers between devices with their start and end apart: 13, of which 9 were waited for; matrix products, arithmetic and copies ran while one was open for 7% of the time, Pallas kernels for 0%

commit v1 on v0

v1 whole, which is shorter than its diff:
```python
import jax
import jax.numpy as jnp
from jax import lax
from jax.sharding import PartitionSpec as P

HEAD_DIM = 64


EPSILON = 1e-05
GELU_COEF = 0.7978845608028654


def gelu_parts(inputs):
    cubed_part = inputs * inputs * inputs
    tanh_part = jnp.tanh(GELU_COEF * (inputs + 0.044715 * cubed_part))
    values = 0.5 * inputs * (1.0 + tanh_part)
    slopes = 0.5 * (1.0 + tanh_part) + 0.5 * inputs * (1.0 - tanh_part * tanh_part) * GELU_COEF * (
        1.0 + 3.0 * 0.044715 * inputs * inputs
    )
    return (values, slopes)


def norm_parts(values):
    centred = values - jnp.mean(values, axis=-1, keepdims=True)
    inverse = lax.rsqrt(jnp.mean(centred * centred, axis=-1, keepdims=True) + EPSILON)
    return (centred * inverse, inverse)


def norm_back(grads, normed, inverse, gain_row):
    scaled = grads * gain_row
    return inverse * (
        scaled
        - jnp.mean(scaled, axis=-1, keepdims=True)
        - normed * jnp.mean(scaled * normed, axis=-1, keepdims=True)
    )


def outer_sum(former, latter):
    return lax.dot_general(
        former, latter, (((0,), (0,)), ((), ())), preferred_element_type=jnp.float32
    )


def back_product(former, latter):
    return lax.dot_general(
        former, latter, (((1,), (1,)), ((), ())), preferred_element_type=jnp.float32
    )


def shards(
    tokens,
    cotangent,
    segment_ids,
    tract_order,
    qkv_weight,
    out_weight,
    up_weight,
    down_weight,
    norm_gain,
    norm_shift,
    proj_bias,
    up_bias,
):
    both = ("dp", "ctx")
    dp_count = lax.axis_size("dp")
    ctx_count = lax.axis_size("ctx")
    here = lax.axis_index("ctx")
    row_count, width = tokens.shape
    span = row_count * ctx_count
    block_rows = segment_ids.shape[1] // tract_order.shape[1]
    own_rows = qkv_weight.shape[0]
    own_hidden = up_bias.shape[0]
    own_feats = norm_gain.shape[1]
    hidden = dp_count * own_hidden
    part = width // ctx_count
    heads = part // HEAD_DIM
    attn_scale = HEAD_DIM ** (-0.5)

    smalls = jnp.concatenate(
        [norm_gain.reshape(-1), norm_shift.reshape(-1), proj_bias.reshape(-1), up_bias]
    )[None]
    smalls = lax.all_gather(smalls, both, axis=0, tiled=True).astype(jnp.float32)

    def spread(first, count):
        piece = smalls[:, first * own_feats : (first + count) * own_feats]
        return piece.reshape(-1, count, own_feats).transpose(1, 0, 2).reshape(count, width)

    gains = spread(0, 2)
    shifts = spread(2, 2)
    biases = spread(4, 4)
    up_shift = lax.dynamic_index_in_dim(
        smalls[:, 8 * own_feats :].reshape(dp_count, ctx_count, own_hidden), here, 1, False
    ).reshape(hidden)

    qkv_cols = (
        qkv_weight.reshape(own_rows, 3, ctx_count, part)
        .transpose(2, 0, 1, 3)
        .reshape(ctx_count, own_rows, 3 * part)
    )
    up_cols = (
        up_weight.reshape(own_rows, dp_count, ctx_count, own_hidden)
        .transpose(2, 0, 1, 3)
        .reshape(ctx_count, own_rows, hidden)
    )
    swapped = lax.all_to_all(
        jnp.concatenate([qkv_cols, up_cols], axis=2), "ctx", 0, 0, tiled=True
    ).reshape(ctx_count * own_rows, 3 * part + hidden)
    streams = lax.all_gather(jnp.stack([tokens, cotangent]), "ctx", axis=1, tiled=True)
    qkv_part = lax.all_gather(swapped[:, : 3 * part], "dp", axis=0, tiled=True)
    out_full = lax.all_gather(out_weight, both, axis=0, tiled=True)
    up_part = lax.all_gather(swapped[:, 3 * part :], "dp", axis=0, tiled=True)
    down_part = lax.all_gather(down_weight, "dp", axis=0, tiled=True)
    tokens_span, cot_span = streams[0], streams[1]

    block_ranks = tract_order[0]
    positions = (
        block_ranks[:, None] * block_rows + jnp.arange(block_rows, dtype=jnp.int32)[None, :]
    ).reshape(-1)
    segments = jnp.take(segment_ids[0].reshape(-1, block_rows), block_ranks, axis=0).reshape(-1)
    allowed = (positions[None, :] <= positions[:, None]) & (
        segments[None, :] == segments[:, None]
    )

    normed_span, _ = norm_parts(tokens_span.astype(jnp.float32))
    normed_in = (normed_span * gains[0] + shifts[0]).astype(jnp.bfloat16)
    projected = jnp.dot(normed_in, qkv_part, preferred_element_type=jnp.float32)
    query_shift = lax.dynamic_slice_in_dim(biases[0], here * part, part)
    value_shift = lax.dynamic_slice_in_dim(biases[1], here * part, part)
    query_heads = (
        (projected[:, :part] + query_shift).astype(jnp.bfloat16).reshape(span, heads, HEAD_DIM)
    )
    key_heads = projected[:, part : 2 * part].astype(jnp.bfloat16).reshape(span, heads, HEAD_DIM)
    value_heads = (
        (projected[:, 2 * part :] + value_shift).astype(jnp.bfloat16).reshape(span, heads, HEAD_DIM)
    )
    scores = (
        jnp.einsum("qhd,khd->hqk", query_heads, key_heads, preferred_element_type=jnp.float32)
        * attn_scale
    )
    exp_weights = jnp.where(allowed[None], jnp.exp(scores), 0.0)
    denominator = jnp.sum(exp_weights, axis=-1)
    numerator = jnp.einsum(
        "hqk,khd->qhd",
        exp_weights.astype(jnp.bfloat16),
        value_heads,
        preferred_element_type=jnp.float32,
    )
    att_heads = (numerator / denominator.T[:, :, None]).astype(jnp.bfloat16)
    log_total = jnp.log(denominator)
    att_part = att_heads.reshape(span, part)
    attended = lax.all_to_all(att_part, "ctx", 0, 1, tiled=True)

    resid_in = tokens.astype(jnp.float32)
    resid_mid = (
        resid_in + jnp.dot(attended, out_full, preferred_element_type=jnp.float32) + biases[2]
    )
    normed_two, inverse_two = norm_parts(resid_mid)
    normed_mid = lax.all_gather(
        (normed_two * gains[1] + shifts[1]).astype(jnp.bfloat16), "ctx", axis=0, tiled=True
    )
    pre_act = jnp.dot(normed_mid, up_part, preferred_element_type=jnp.float32) + up_shift
    activated, slopes = gelu_parts(pre_act)
    act_rows = activated.astype(jnp.bfloat16)

    grad_top = cotangent.astype(jnp.float32)
    grad_act = back_product(cot_span, down_part)
    grad_pre = grad_act * slopes
    grad_pre_low = grad_pre.astype(jnp.bfloat16)
    grad_norm_two = lax.psum_scatter(
        back_product(grad_pre_low, up_part).astype(jnp.bfloat16),
        "ctx",
        scatter_dimension=0,
        tiled=True,
    ).astype(jnp.float32)
    block_out = (
        resid_mid
        + lax.psum_scatter(
            jnp.dot(act_rows, down_part, preferred_element_type=jnp.float32).astype(jnp.bfloat16),
            "ctx",
            scatter_dimension=0,
            tiled=True,
        ).astype(jnp.float32)
        + biases[3]
    )
    grad_mid = grad_top + norm_back(grad_norm_two, normed_two, inverse_two, gains[1])
    mid_span = lax.all_gather(grad_mid.astype(jnp.bfloat16), "ctx", axis=0, tiled=True)
    out_rows = lax.dynamic_slice_in_dim(out_full, here * part, part)
    grad_att = back_product(mid_span, out_rows).astype(jnp.bfloat16).reshape(span, heads, HEAD_DIM)
    delta_rows = jnp.sum(
        grad_att.astype(jnp.float32) * att_heads.astype(jnp.float32), axis=-1
    ).T
    soft_weights = jnp.where(allowed[None], jnp.exp(scores - log_total[:, :, None]), 0.0)
    grad_value = jnp.einsum(
        "hqk,qhd->khd",
        soft_weights.astype(jnp.bfloat16),
        grad_att,
        preferred_element_type=jnp.float32,
    ).reshape(span, part)
    grad_probs = jnp.einsum(
        "qhd,khd->hqk", grad_att, value_heads, preferred_element_type=jnp.float32
    )
    grad_scores = (soft_weights * (grad_probs - delta_rows[:, :, None])).astype(jnp.bfloat16)
    grad_query = (
        jnp.einsum(
            "hqk,khd->qhd", grad_scores, key_heads, preferred_element_type=jnp.float32
        ).reshape(span, part)
        * attn_scale
    )
    grad_key = (
        jnp.einsum(
            "hqk,qhd->khd", grad_scores, query_heads, preferred_element_type=jnp.float32
        ).reshape(span, part)
        * attn_scale
    )
    grad_proj = jnp.concatenate([grad_query, grad_key, grad_value], axis=1).astype(jnp.bfloat16)
    grad_norm_one = lax.psum_scatter(
        back_product(grad_proj, qkv_part).astype(jnp.bfloat16),
        "ctx",
        scatter_dimension=0,
        tiled=True,
    ).astype(jnp.float32)
    normed_one, inverse_one = norm_parts(resid_in)
    input_grad = grad_mid + norm_back(grad_norm_one, normed_one, inverse_one, gains[0])

    def over_dp(former, latter):
        return lax.psum_scatter(
            outer_sum(former, latter).astype(jnp.bfloat16), "dp", scatter_dimension=0, tiled=True
        )

    down_grad = over_dp(act_rows, cot_span).astype(jnp.float32)
    up_rows = over_dp(normed_mid, grad_pre_low)
    outw_rows = over_dp(att_part, mid_span)
    qkv_rows = over_dp(normed_in, grad_proj)
    outw_grad = lax.ppermute(
        outw_rows,
        both,
        [
            (d * ctx_count + c, c * dp_count + d)
            for d in range(dp_count)
            for c in range(ctx_count)
        ],
    ).astype(jnp.float32)
    returned = lax.all_to_all(
        jnp.concatenate([qkv_rows, up_rows], axis=1).reshape(ctx_count, own_rows, -1),
        "ctx",
        0,
        0,
        tiled=True,
    ).astype(jnp.float32)
    qkv_grad = (
        returned[:, :, : 3 * part]
        .reshape(ctx_count, own_rows, 3, part)
        .transpose(1, 2, 0, 3)
        .reshape(own_rows, 3 * width)
    )
    up_grad = (
        returned[:, :, 3 * part :]
        .reshape(ctx_count, own_rows, dp_count, own_hidden)
        .transpose(1, 2, 0, 3)
        .reshape(own_rows, hidden * ctx_count)
    )

    def placed(sums):
        return lax.dynamic_update_slice_in_dim(
            jnp.zeros((width,), jnp.float32), sums, here * part, 0
        )

    feature_sums = jnp.stack(
        [
            jnp.sum(grad_norm_one * normed_one, axis=0),
            jnp.sum(grad_norm_two * normed_two, axis=0),
            jnp.sum(grad_norm_one, axis=0),
            jnp.sum(grad_norm_two, axis=0),
            placed(jnp.sum(grad_query, axis=0)),
            placed(jnp.sum(grad_value, axis=0)),
            jnp.sum(grad_mid, axis=0),
            jnp.sum(grad_top, axis=0),
        ]
    )
    hidden_sums = lax.dynamic_update_slice_in_dim(
        jnp.zeros((dp_count, ctx_count, own_hidden), jnp.float32),
        jnp.sum(grad_pre, axis=0).reshape(dp_count, 1, own_hidden),
        here,
        1,
    ).reshape(dp_count * ctx_count, own_hidden)
    packed = jnp.concatenate(
        [
            feature_sums.reshape(8, -1, own_feats).transpose(1, 0, 2).reshape(-1, 8 * own_feats),
            hidden_sums,
        ],
        axis=1,
    )
    owned = lax.psum_scatter(packed, both, scatter_dimension=0, tiled=True)[0]
    rows = owned[: 8 * own_feats].reshape(8, own_feats)
    return (
        block_out,
        input_grad,
        qkv_grad,
        outw_grad,
        up_grad,
        down_grad,
        rows[0:2],
        rows[2:4],
        rows[4:8],
        owned[8 * own_feats :],
    )


def solution(mesh):
    return jax.shard_map(
        shards,
        mesh=mesh,
        in_specs=(
            P(("dp", "ctx"), None),
            P(("dp", "ctx"), None),
            P("dp", None),
            P("dp", None),
            P(("dp", "ctx"), None),
            P(("dp", "ctx"), None),
            P(("dp", "ctx"), None),
            P(("dp", "ctx"), None),
            P(None, ("dp", "ctx")),
            P(None, ("dp", "ctx")),
            P(None, ("dp", "ctx")),
            P(("dp", "ctx")),
        ),
        out_specs=(
            P(("dp", "ctx"), None),
            P(("dp", "ctx"), None),
            P(("dp", "ctx"), None),
            P(("dp", "ctx"), None),
            P(("dp", "ctx"), None),
            P(("dp", "ctx"), None),
            P(None, ("dp", "ctx")),
            P(None, ("dp", "ctx")),
            P(None, ("dp", "ctx")),
            P(("dp", "ctx")),
        ),
        check_vma=False,
    )
```

time: 1410 us -> 667 us (0.47)
  waiting for transfers between devices: 1050 us -> 459 us
  blocking collectives: 195 us -> 94.7 us
  matrix products: 82.4 us -> 47.9 us
    unnamed x18 -> x14, waiting for transfers between devices: 344 us -> 1.4 us
    reduce_scatter x2 -> x7, waiting for transfers between devices: 535 us -> 272 us  [the longest x4 204 us: over_dp(): lax.psum_scatter(outer_sum(former, latter).astype(jnp.bfloat16), 'dp', sc...]
    all_gather x4 -> x1, blocking collectives: 156 us -> 40.8 us  [shards(): lax.all_gather(smalls, both, axis=0, tiled=True).astype(jnp.float32)]
    concatenate x1 -> x4, other arithmetic: 22.8 us -> 1.92 us  [the longest x1 1.8 us: shards(): jnp.concatenate([qkv_rows, up_rows], axis=1)]
    all_gather x6 -> x7, waiting for transfers between devices: 171 us -> 176 us  [the longest x1 46.5 us: shards(): down_part = lax.all_gather(down_weight, 'dp', axis=0, tiled=True)]
  transfers between devices with their start and end apart: 13 -> 17, of which waited for: 9 -> 15; matrix products, arithmetic and copies ran while one was open for 7% -> 10% of each run, Pallas kernels for 0% -> 0%
where the time goes in v1:
time: 667 us; the launch traced here: 666 us
  waiting for transfers between devices  459 us (69%)
  blocking collectives  94.7 us (14%)
  matrix products  47.9 us (7%)
  local copies, waits for them, and re-layouts  20.1 us (3%)
  other arithmetic  20 us (3%)
  between operations  14.6 us (2%)
  starting transfers between devices  9.33 us (1%)
    reduce_scatter x4, waiting for transfers between devices, over_dp(): lax.psum_scatter(outer_sum(former, latter).astype(jnp.bfloat16), 'dp', sc...  204 us
    all_gather x1, waiting for transfers between devices, shards(): down_part = lax.all_gather(down_weight, 'dp', axis=0, tiled=True)  46.5 us
    all_gather x1, waiting for transfers between devices, shards(): up_part = lax.all_gather(swapped[:, 3 * part:], 'dp', axis=0, tiled=True)  46.4 us
    all_gather x1, blocking collectives, shards(): lax.all_gather(smalls, both, axis=0, tiled=True).astype(jnp.float32)  40.8 us
    unnamed x1, blocking collectives  40.7 us
    all_gather x1, waiting for transfers between devices, shards(): out_full = lax.all_gather(out_weight, both, axis=0, tiled=True)  40.1 us
    reduce_scatter x1, waiting for transfers between devices, shards(): lax.psum_scatter(jnp.dot(act_rows, down_part, preferred_element_type=jnp....  26.1 us
    reduce_scatter x1, waiting for transfers between devices, shards(): lax.psum_scatter(back_product(grad_proj, qkv_part).astype(jnp.bfloat16),...  23.7 us
  transfers between devices with their start and end apart: 17, of which 15 were waited for; matrix products, arithmetic and copies ran while one was open for 10% of the time, Pallas kernels for 0%

profile of v1, /device:TPU:0, one launch (start us, length us, event | category | flops | bytes accessed | tf_op | source)
XLA Modules:
  0.0 666.1 jit_solution(16236123342175305526)
XLA Ops:
  7.2 1.9 pad_maximum_fusion.1
  9.2 1.1 reshape.376
  11.1 13.2 %all_to_all.29 = bf16[4,32,1792]{2,1,0:T(8,128)(2,1)S(1)} all-to-all(bf16[4,32,1792]{2,1,0:T(8,128)(2,1)S(1)} %pad_maximum_fusion.2), channel_id=1, replica_groups=mesh['dp'=8,'ctx'=4] {'ctx'}, dimensions={0} | all-to-all | bytes 917504 | tf_op jit(solution)/shard_map/all_to_all | solution.py:105
  26.2 40.8 %all-gather.1 = bf16[32,1,384]{2,1,0:T(2,128)(2,1)S(1)} all-gather(bf16[1,1,384]{2,1,0:T(2,128)(2,1)S(1)} %reshape.405), channel_id=2, replica_groups=mesh['dp'=8,'ctx'=4] {'dp','ctx'}, dimensions={0}, use_global_device_ids=true | all-gather | bytes 25344 | tf_op jit(solution)/shard_map/all_gather | solution.py:82
  71.4 1.6 convert_reduce_fusion
  73.0 1.6 fusion.6
  74.7 8.8 %all-gather.12.cloned.1.call-done = bf16[1024,768]{1,0:T(8,128)(2,1)} async-done(((bf16[128,768]{1,0:T(8,128)(2,1)}), bf16[1024,768]{1,0:T(8,128)(2,1)}) %all-gather.12.cloned.1.call-update) | async-done | bytes 1572880 | tf_op jit(solution)/shard_map/all_gather | solution.py:109
  83.5 2.5 fusion.73
  86.6 1.3 fusion
  88.0 1.9 copy-done.24
  91.6 3.4 all-to-all-start.1
  95.3 5.7 all-to-all-done.1
  101.0 40.1 %all-gather.14.cloned.1.call-done = bf16[1024,1024]{1,0:T(8,128)(2,1)} async-done(((bf16[32,1024]{1,0:T(8,128)(2,1)}), bf16[1024,1024]{1,0:T(8,128)(2,1)}) %all-gather.14.cloned.1.call-update) | async-done | bytes 2097168 | tf_op jit(solution)/shard_map/all_gather | solution.py:110
  141.1 2.1 fusion.80
  145.2 46.4 %all-gather.18.cloned.1.call-done = bf16[1024,1024]{1,0:T(8,128)(2,1)} async-done(((bf16[128,1024]{1,0:T(8,128)(2,1)}), bf16[1024,1024]{1,0:T(8,128)(2,1)}) %all-gather.18.cloned.1.call-update) | async-done | bytes 2097168 | tf_op jit(solution)/shard_map/all_gather | solution.py:111
  191.6 17.2 %all-gather.16.cloned.1.call-done = bf16[512,1024]{1,0:T(8,128)(2,1)} async-done(((bf16[128,1024]{1,0:T(8,128)(2,1)}), bf16[512,1024]{1,0:T(8,128)(2,1)}) %all-gather.16.cloned.1.call-update) | async-done | bytes 1048592 | tf_op jit(solution)/shard_map/all_gather | solution.py:158
  208.9 4.6 fusion.82
  213.4 46.5 %all-gather.20.cloned.1.call-done = bf16[1024,1024]{1,0:T(8,128)(2,1)} async-done(((bf16[128,1024]{1,0:T(8,128)(2,1)}), bf16[1024,1024]{1,0:T(8,128)(2,1)}) %all-gather.20.cloned.1.call-update) | async-done | bytes 2097168 | tf_op jit(solution)/shard_map/all_gather | solution.py:112
  260.0 4.8 fusion.81
  265.8 2.3 convolution_convert_fusion.4
  268.1 4.7 convolution_convert_fusion.5
  273.0 18.6 %reduce-scatter.10.cloned.1.call-done = bf16[128,1024]{1,0:T(8,128)(2,1)} async-done(((bf16[512,1024]{1,0:T(8,128)(2,1)}), bf16[128,1024]{1,0:T(8,128)(2,1)}) %reduce-scatter.10.cloned.1.call-update) | async-done | bytes 262160 | tf_op jit(solution)/shard_map/reduce_scatter | solution.py:169
  291.5 1.2 fusion.57
  292.8 26.1 %reduce-scatter.8.cloned.1.call-done = bf16[128,1024]{1,0:T(8,128)(2,1)} async-done(((bf16[512,1024]{1,0:T(8,128)(2,1)}), bf16[128,1024]{1,0:T(8,128)(2,1)}) %reduce-scatter.8.cloned.1.call-update) | async-done | bytes 262160 | tf_op jit(solution)/shard_map/reduce_scatter | solution.py:177
  318.9 2.2 fusion.75
  321.9 16.8 %all-gather.22.cloned.1.call-done = bf16[512,1024]{1,0:T(8,128)(2,1)} async-done(((bf16[128,1024]{1,0:T(8,128)(2,1)}), bf16[512,1024]{1,0:T(8,128)(2,1)}) %all-gather.22.cloned.1.call-update) | async-done | bytes 1048592 | tf_op jit(solution)/shard_map/all_gather | solution.py:186
  338.7 2.5 convolution_convert_fusion.6
  341.3 4.6 convolution_convert_fusion
  346.8 1.9 multiply_reduce_fusion
  348.7 3.8 multiply_convert_fusion
  354.9 1.1 fusion.76
  356.7 2.0 convolution_convert_fusion.3
  358.8 4.2 convolution_convert_fusion.1
  363.0 3.4 convolution_convert_fusion.2
  368.6 36.6 %reduce-scatter.18.cloned.1.call-done = bf16[32,1024]{1,0:T(8,128)(2,1)} async-done(((bf16[256,1024]{1,0:T(8,128)(2,1)}), bf16[32,1024]{1,0:T(8,128)(2,1)}) %reduce-scatter.18.cloned.1.call-update) | async-done | bytes 65552 | tf_op jit(solution)/shard_map/reduce_scatter | solution.py:226
  405.2 1.5 collective-permute-start
  407.5 68.8 %reduce-scatter.20.cloned.1.call-done = bf16[128,1024]{1,0:T(8,128)(2,1)} async-done(((bf16[1024,1024]{1,0:T(8,128)(2,1)}), bf16[128,1024]{1,0:T(8,128)(2,1)}) %reduce-scatter.20.cloned.1.call-update) | async-done | bytes 262160 | tf_op jit(solution)/shard_map/reduce_scatter | solution.py:226
  476.3 1.8 convert_element_type.129
  478.7 23.7 %reduce-scatter.12.cloned.1.call-done = bf16[128,1024]{1,0:T(8,128)(2,1)} async-done(((bf16[512,1024]{1,0:T(8,128)(2,1)}), bf16[128,1024]{1,0:T(8,128)(2,1)}) %reduce-scatter.12.cloned.1.call-update) | async-done | bytes 262160 | tf_op jit(solution)/shard_map/reduce_scatter | solution.py:216
  502.5 1.3 fusion.58
  504.3 40.7 %all-reduce = f32[32,384]{1,0:T(8,128)S(1)} all-reduce(f32[32,384]{1,0:T(8,128)S(1)} %pad_maximum_fusion.6), channel_id=10, replica_groups=mesh['dp'=8,'ctx'=4] {'dp','ctx'}, use_global_device_ids=true, to_apply=%region_28.29.clone | all-reduce | flops 12288 | bytes 98304
  545.0 30.5 %reduce-scatter.16.cloned.1.call-done = bf16[128,1024]{1,0:T(8,128)(2,1)} async-done(((bf16[1024,1024]{1,0:T(8,128)(2,1)}), bf16[128,1024]{1,0:T(8,128)(2,1)}) %reduce-scatter.16.cloned.1.call-update) | async-done | bytes 262160 | tf_op jit(solution)/shard_map/reduce_scatter | solution.py:226
  575.4 67.8 %reduce-scatter.14.cloned.1.call-done = bf16[128,768]{1,0:T(8,128)(2,1)} async-done(((bf16[1024,768]{1,0:T(8,128)(2,1)}), bf16[128,768]{1,0:T(8,128)(2,1)}) %reduce-scatter.14.cloned.1.call-update) | async-done | bytes 196624 | tf_op jit(solution)/shard_map/reduce_scatter | solution.py:226
  643.2 1.8 pad_maximum_fusion.3
  645.0 3.5 all-to-all-start.2
  651.1 1.0 fusion.51
  652.2 4.4 all-to-all-done.2
  657.1 1.0 reshape.391
  (189 shorter events, 26.2 us)
Async XLA Ops:
  7.2 3.4 copy-start.14
  7.2 64.2 %all-gather.10.cloned.1.call-start = ((), (), s32[]{:S(2)}) async-start(), calls=%async_computation.10 | async-start | bytes 2621440 | tf_op jit(solution)/shard_map/all_gather | solution.py:108
  9.2 74.3 %all-gather.12.cloned.1.call-start = ((), (), s32[]{:S(2)}) async-start(), calls=%async_computation.11 | async-start | bytes 1769472 | tf_op jit(solution)/shard_map/all_gather | solution.py:109
  10.4 15.4 %copy-start.20 = (bf16[2,32]{1,0:T(2,128)(2,1)S(1)}, bf16[2,32]{1,0:T(2,128)(2,1)}, u32[]{:S(2)}) copy-start(bf16[2,32]{1,0:T(2,128)(2,1)} %param.20) | copy-start | bytes 388
  10.4 15.5 %copy-start.21 = (bf16[2,32]{1,0:T(2,128)(2,1)S(1)}, bf16[2,32]{1,0:T(2,128)(2,1)}, u32[]{:S(2)}) copy-start(bf16[2,32]{1,0:T(2,128)(2,1)} %param.21) | copy-start | bytes 388
  10.4 15.6 %copy-start.19 = (bf16[4,32]{1,0:T(4,128)(2,1)S(1)}, bf16[4,32]{1,0:T(4,128)(2,1)}, u32[]{:S(2)}) copy-start(bf16[4,32]{1,0:T(4,128)(2,1)} %param.22) | copy-start | bytes 772
  10.4 15.7 %copy-start.16 = (bf16[128]{0:T(256)(128)(2,1)S(1)}, bf16[128]{0:T(256)(128)(2,1)}, u32[]{:S(2)}) copy-start(bf16[128]{0:T(256)(128)(2,1)} %param.23) | copy-start | bytes 772
  10.7 58.0 %copy-start.15 = (s32[1,512]{1,0:T(1,128)S(1)}, s32[1,512]{1,0:T(1,128)}, u32[]{:S(2)}) copy-start(s32[1,512]{1,0:T(1,128)} %param.14) | copy-start | bytes 6148
  10.7 58.7 %copy-start.22 = (s32[1,8]{1,0:T(1,128)S(1)}, s32[1,8]{1,0:T(1,128)}, u32[]{:S(2)}) copy-start(s32[1,8]{1,0:T(1,128)} %param.15) | copy-start | bytes 100
  25.0 116.1 %all-gather.14.cloned.1.call-start = ((), (), s32[]{:S(2)}) async-start(), calls=%async_computation.12 | async-start | bytes 2162688 | tf_op jit(solution)/shard_map/all_gather | solution.py:110
  25.8 165.8 %all-gather.18.cloned.1.call-start = ((), (), s32[]{:S(2)}) async-start(), calls=%async_computation.14 | async-start | bytes 2359296 | tf_op jit(solution)/shard_map/all_gather | solution.py:111
  71.4 16.6 %copy-start.9 = (pred[512,512]{0,1:T(8,128)(4,1)}, pred[512,512]{0,1:T(8,128)(4,1)S(1)}, u32[]{:S(2)}) copy-start(pred[512,512]{0,1:T(8,128)(4,1)S(1)} %compare_and_fusion) | copy-start | bytes 786436
  71.4 12.0 %copy-start.1 = (bf16[2,512,1024]{2,1,0:T(8,128)(2,1)S(1)}, bf16[2,512,1024]{2,1,0:T(8,128)(2,1)}, u32[]{:S(2)}) copy-start(bf16[2,512,1024]{2,1,0:T(8,128)(2,1)} %all-gather.10.cloned.1.call-done) | copy-start | bytes 6291460
  86.3 1.6 copy-start.2
  86.5 1.5 copy-start.4
  86.6 1.4 copy-start.12
  88.0 1.9 copy-start.24
  89.9 51.2 %copy-start = (bf16[128,1024]{1,0:T(8,128)(2,1)S(1)}, bf16[128,1024]{1,0:T(8,128)(2,1)}, u32[]{:S(2)}) copy-start(bf16[128,1024]{1,0:T(8,128)(2,1)} %param.12) | copy-start | bytes 786436
  90.8 52.4 %copy-start.6 = (bf16[512,4,64]{0,2,1:T(8,128)(2,1)}, bf16[512,4,64]{0,2,1:T(8,128)(2,1)S(1)}, u32[]{:S(2)}) copy-start(bf16[512,4,64]{0,2,1:T(8,128)(2,1)S(1)} %fusion.37) | copy-start | bytes 786436
  91.6 9.4 %all-to-all-start.1 = ((bf16[4,128,256]{1,2,0:T(8,128)(2,1)}), bf16[4,128,256]{1,2,0:T(8,128)(2,1)S(1)}, u32[]{:S(2)}, u32[]{:S(2)}) async-start(bf16[4,128,256]{1,2,0:T(8,128)(2,1)} %copy.66), calls=%async_computation.1 | async-start | bytes 524288 | tf_op jit(solution)/shard_map/all_to_all | solution.py:151
  95.0 113.8 %all-gather.16.cloned.1.call-start = ((), (), s32[]{:S(2)}) async-start(), calls=%async_computation.13 | async-start | bytes 1310720 | tf_op jit(solution)/shard_map/all_gather | solution.py:158
  144.4 115.6 %all-gather.20.cloned.1.call-start = ((), (), s32[]{:S(2)}) async-start(), calls=%async_computation.15 | async-start | bytes 2359296 | tf_op jit(solution)/shard_map/all_gather | solution.py:112
  144.9 146.6 %reduce-scatter.10.cloned.1.call-start = ((), (), s32[]{:S(2)}) async-start(), calls=%async_computation.17 | async-start | bytes 1310720 | tf_op jit(solution)/shard_map/reduce_scatter | solution.py:169
  260.0 5.8 copy-start.17
  264.7 1.0 copy-start.26
  268.1 50.8 %reduce-scatter.8.cloned.1.call-start = ((), (), s32[]{:S(2)}) async-start(), calls=%async_computation.16 | async-start | bytes 1310720 | tf_op jit(solution)/shard_map/reduce_scatter | solution.py:177
  272.9 65.8 %all-gather.22.cloned.1.call-start = ((), (), s32[]{:S(2)}) async-start(), calls=%async_computation.18 | async-start | bytes 1310720 | tf_op jit(solution)/shard_map/all_gather | solution.py:186
  321.8 83.4 %reduce-scatter.18.cloned.1.call-start = ((), (), s32[]{:S(2)}) async-start(), calls=%async_computation.22 | async-start | bytes 589824 | tf_op jit(solution)/shard_map/reduce_scatter | solution.py:226
  341.2 135.0 %reduce-scatter.20.cloned.1.call-start = ((), (), s32[]{:S(2)}) async-start(), calls=%async_computation.23 | async-start | bytes 2359296 | tf_op jit(solution)/shard_map/reduce_scatter | solution.py:226
  345.9 0.9 copy-start.7
  345.9 2.8 copy-start.10
  345.9 156.6 %reduce-scatter.12.cloned.1.call-start = ((), (), s32[]{:S(2)}) async-start(), calls=%async_computation.19 | async-start | bytes 1310720 | tf_op jit(solution)/shard_map/reduce_scatter | solution.py:216
  346.2 2.5 copy-start.13
  348.7 3.8 copy-start.5
  352.5 1.0 copy-start.3
  352.5 1.7 copy-start.11
  352.5 2.3 copy-start.25
  354.9 1.8 copy-start.18
  356.0 0.7 copy-start.23
  358.7 216.7 %reduce-scatter.16.cloned.1.call-start = ((), (), s32[]{:S(2)}) async-start(), calls=%async_computation.21 | async-start | bytes 2359296 | tf_op jit(solution)/shard_map/reduce_scatter | solution.py:226
  363.0 280.2 %reduce-scatter.14.cloned.1.call-start = ((), (), s32[]{:S(2)}) async-start(), calls=%async_computation.20 | async-start | bytes 1769472 | tf_op jit(solution)/shard_map/reduce_scatter | solution.py:226
  405.2 72.8 %collective-permute-start = (bf16[32,1024]{1,0:T(8,128)(2,1)}, bf16[32,1024]{1,0:T(8,128)(2,1)S(1)}, u32[]{:S(2)}, u32[]{:S(2)}) collective-permute-start(bf16[32,1024]{1,0:T(8,128)(2,1)} %reduce-scatter.18.cloned.1.call-done), channel_id=1, source_target_pairs={{0,0},{1,8},{2,16},{3,24},{4,1},{5,9},{6,17},{7,25},{8,2},{9,10},{... | collective-permute-start | bytes 196616 | tf_op jit(solution)/shard_map/ppermute | solution.py:234
  502.5 148.7 %copy-start.8 = (bf16[128,1024]{1,0:T(8,128)(2,1)S(1)}, bf16[128,1024]{1,0:T(8,128)(2,1)}, u32[]{:S(2)}) copy-start(bf16[128,1024]{1,0:T(8,128)(2,1)} %reduce-scatter.12.cloned.1.call-done) | copy-start | bytes 786436
  645.0 11.6 %all-to-all-start.2 = ((bf16[4,32,1792]{2,1,0:T(8,128)(2,1)}), bf16[4,32,1792]{2,1,0:T(8,128)(2,1)S(1)}, u32[]{:S(2)}, u32[]{:S(2)}) async-start(bf16[4,32,1792]{2,1,0:T(8,128)(2,1)} %bitcast.30), calls=%async_computation.7 | async-start | bytes 917504 | tf_op jit(solution)/shard_map/all_to_all | solution.py:243
Sparse Core Ops, SparseCore 0:
  10.1 25.9 all-gather.9
  38.8 44.5 all-gather.11
  86.3 54.7 all-gather.13
  143.6 47.9 all-gather.17
  193.6 15.2 all-gather.15
  210.8 49.0 all-gather.19
  268.2 23.2 reduce-scatter.9
  294.1 24.7 reduce-scatter.7
  321.9 16.6 all-gather.21
  342.4 62.7 reduce-scatter.17
  408.8 67.4 reduce-scatter.19
  478.6 23.7 reduce-scatter.11
  506.0 69.3 reduce-scatter.15
  578.7 64.4 reduce-scatter.13

commit v2 on v1

--- a/solution.py
+++ b/solution.py
@@ -45,6 +45,16 @@
     return lax.dot_general(
         former, latter, (((1,), (1,)), ((), ())), preferred_element_type=jnp.float32
     )
+
+
+def shared(rows, axis, count):
+    spread_rows = jnp.broadcast_to(rows[None], (count,) + rows.shape)
+    return lax.all_to_all(spread_rows, axis, 0, 0, tiled=True).reshape((-1,) + rows.shape[1:])
+
+
+def summed(partial, axis, count):
+    parts = lax.all_to_all(partial, axis, 0, 0, tiled=True)
+    return jnp.sum(parts.reshape((count, -1) + partial.shape[1:]).astype(jnp.float32), axis=0)
 
 
 def shards(
@@ -79,7 +89,7 @@
     smalls = jnp.concatenate(
         [norm_gain.reshape(-1), norm_shift.reshape(-1), proj_bias.reshape(-1), up_bias]
     )[None]
-    smalls = lax.all_gather(smalls, both, axis=0, tiled=True).astype(jnp.float32)
+    smalls = shared(smalls, both, dp_count * ctx_count).astype(jnp.float32)
 
     def spread(first, count):
         piece = smalls[:, first * own_feats : (first + count) * own_feats]
@@ -105,12 +115,18 @@
     swapped = lax.all_to_all(
         jnp.concatenate([qkv_cols, up_cols], axis=2), "ctx", 0, 0, tiled=True
     ).reshape(ctx_count * own_rows, 3 * part + hidden)
-    streams = lax.all_gather(jnp.stack([tokens, cotangent]), "ctx", axis=1, tiled=True)
-    qkv_part = lax.all_gather(swapped[:, : 3 * part], "dp", axis=0, tiled=True)
-    out_full = lax.all_gather(out_weight, both, axis=0, tiled=True)
+    tokens_span = shared(tokens, "ctx", ctx_count)
+    cot_span = shared(cotangent, "ctx", ctx_count)
+    qkv_part = shared(swapped[:, : 3 * part], "dp", dp_count)
+    out_part = lax.all_gather(out_weight, "dp", axis=0, tiled=True)
+    out_full = (
+        shared(out_part, "ctx", ctx_count)
+        .reshape(ctx_count, dp_count, own_rows, width)
+        .transpose(1, 0, 2, 3)
+        .reshape(width, width)
+    )
     up_part = lax.all_gather(swapped[:, 3 * part :], "dp", axis=0, tiled=True)
     down_part = lax.all_gather(down_weight, "dp", axis=0, tiled=True)
-    tokens_span, cot_span = streams[0], streams[1]
 
     block_ranks = tract_order[0]
     positions = (
@@ -155,8 +171,8 @@
         resid_in + jnp.dot(attended, out_full, preferred_element_type=jnp.float32) + biases[2]
     )
     normed_two, inverse_two = norm_parts(resid_mid)
-    normed_mid = lax.all_gather(
-        (normed_two * gains[1] + shifts[1]).astype(jnp.bfloat16), "ctx", axis=0, tiled=True
+    normed_mid = shared(
+        (normed_two * gains[1] + shifts[1]).astype(jnp.bfloat16), "ctx", ctx_count
     )
     pre_act = jnp.dot(normed_mid, up_part, preferred_element_type=jnp.float32) + up_shift
     activated, slopes = gelu_parts(pre_act)
@@ -166,24 +182,20 @@
     grad_act = back_product(cot_span, down_part)
     grad_pre = grad_act * slopes
     grad_pre_low = grad_pre.astype(jnp.bfloat16)
-    grad_norm_two = lax.psum_scatter(
-        back_product(grad_pre_low, up_part).astype(jnp.bfloat16),
-        "ctx",
-        scatter_dimension=0,
-        tiled=True,
-    ).astype(jnp.float32)
+    grad_norm_two = summed(
+        back_product(grad_pre_low, up_part).astype(jnp.bfloat16), "ctx", ctx_count
+    )
     block_out = (
         resid_mid
-        + lax.psum_scatter(
+        + summed(
             jnp.dot(act_rows, down_part, preferred_element_type=jnp.float32).astype(jnp.bfloat16),
             "ctx",
-            scatter_dimension=0,
-            tiled=True,
-        ).astype(jnp.float32)
+            ctx_count,
+        )
         + biases[3]
     )
     grad_mid = grad_top + norm_back(grad_norm_two, normed_two, inverse_two, gains[1])
-    mid_span = lax.all_gather(grad_mid.astype(jnp.bfloat16), "ctx", axis=0, tiled=True)
+    mid_span = shared(grad_mid.astype(jnp.bfloat16), "ctx", ctx_count)
     out_rows = lax.dynamic_slice_in_dim(out_full, here * part, part)
     grad_att = back_product(mid_span, out_rows).astype(jnp.bfloat16).reshape(span, heads, HEAD_DIM)
     delta_rows = jnp.sum(
@@ -213,12 +225,9 @@
         * attn_scale
     )
     grad_proj = jnp.concatenate([grad_query, grad_key, grad_value], axis=1).astype(jnp.bfloat16)
-    grad_norm_one = lax.psum_scatter(
-        back_product(grad_proj, qkv_part).astype(jnp.bfloat16),
-        "ctx",
-        scatter_dimension=0,
-        tiled=True,
-    ).astype(jnp.float32)
+    grad_norm_one = summed(
+        back_product(grad_proj, qkv_part).astype(jnp.bfloat16), "ctx", ctx_count
+    )
     normed_one, inverse_one = norm_parts(resid_in)
     input_grad = grad_mid + norm_back(grad_norm_one, normed_one, inverse_one, gains[0])
 
@@ -228,9 +237,13 @@
         )
 
     down_grad = over_dp(act_rows, cot_span).astype(jnp.float32)
-    up_rows = over_dp(normed_mid, grad_pre_low)
+    up_rows = summed(
+        outer_sum(normed_mid, grad_pre_low).astype(jnp.bfloat16), "dp", dp_count
+    ).astype(jnp.bfloat16)
     outw_rows = over_dp(att_part, mid_span)
-    qkv_rows = over_dp(normed_in, grad_proj)
+    qkv_rows = summed(
+        outer_sum(normed_in, grad_proj).astype(jnp.bfloat16), "dp", dp_count
+    ).astype(jnp.bfloat16)
     outw_grad = lax.ppermute(
         outw_rows,
         both,
@@ -290,7 +303,7 @@
         ],
         axis=1,
     )
-    owned = lax.psum_scatter(packed, both, scatter_dimension=0, tiled=True)[0]
+    owned = summed(packed, both, dp_count * ctx_count)[0]
     rows = owned[: 8 * own_feats].reshape(8, own_feats)
     return (
         block_out,

time: 667 us -> 502 us (0.75)
  waiting for transfers between devices: 459 us -> 214 us
  starting transfers between devices: 9.33 us -> 51.6 us
  local copies, waits for them, and re-layouts: 20.1 us -> 43.9 us
  blocking collectives: 94.7 us -> 109 us
    all_to_all x0 -> x11, waiting for transfers between devices: none -> 154 us  [the longest x6 112 us: summed(): parts = lax.all_to_all(partial, axis, 0, 0, tiled=True)]
    reduce_scatter x4 -> x2, waiting for transfers between devices: 204 us -> 54.6 us  [over_dp(): lax.psum_scatter(outer_sum(former, latter).astype(jnp.bfloat16), 'dp', sc...]
    all_gather x5 -> x0, waiting for transfers between devices: 82.9 us -> none  [the longest x1 40.1 us: shards(): out_full = lax.all_gather(out_weight, both, axis=0, tiled=True)]
    reduce_scatter x3 -> x0, waiting for transfers between devices: 68.4 us -> none  [the longest x1 26.1 us: shards(): lax.psum_scatter(jnp.dot(act_rows, down_part, preferred_element_type=jnp....]
    all_gather x1, waiting for transfers between devices: 46.5 us -> 0.01 us  [shards(): down_part = lax.all_gather(down_weight, 'dp', axis=0, tiled=True)]
    all_gather x1, waiting for transfers between devices: 46.4 us -> 0.01 us  [shards(): up_part = lax.all_gather(swapped[:, 3 * part:], 'dp', axis=0, tiled=True)]
    all_to_all x0 -> x11, starting transfers between devices: none -> 42.5 us  [the longest x6 24.4 us: summed(): parts = lax.all_to_all(partial, axis, 0, 0, tiled=True)]
    unnamed x1 -> x0, blocking collectives: 40.7 us -> none
  transfers between devices with their start and end apart: 17 -> 18, of which waited for: 15 -> 12; matrix products, arithmetic and copies ran while one was open for 10% -> 15% of each run, Pallas kernels for 0% -> 0%
where the time goes in v2:
time: 502 us; the launch traced here: 499 us
  waiting for transfers between devices  214 us (43%)
  blocking collectives  109 us (22%)
  starting transfers between devices  51.6 us (10%)
  matrix products  46.1 us (9%)
  local copies, waits for them, and re-layouts  43.9 us (9%)
  other arithmetic  20.2 us (4%)
  between operations  14.5 us (3%)
    all_to_all x6, waiting for transfers between devices, summed(): parts = lax.all_to_all(partial, axis, 0, 0, tiled=True)  112 us
    all_gather x1, blocking collectives, shards(): out_part = lax.all_gather(out_weight, 'dp', axis=0, tiled=True)  67.3 us
    reduce_scatter x2, waiting for transfers between devices, over_dp(): lax.psum_scatter(outer_sum(former, latter).astype(jnp.bfloat16), 'dp', sc...  54.6 us
    all_to_all x5, waiting for transfers between devices, shared(): lax.all_to_all(spread_rows, axis, 0, 0, tiled=True)  42 us
    all_to_all x2, blocking collectives, shared(): lax.all_to_all(spread_rows, axis, 0, 0, tiled=True)  29.5 us
    all_to_all x6, starting transfers between devices, summed(): parts = lax.all_to_all(partial, axis, 0, 0, tiled=True)  24.4 us
    all_to_all x5, starting transfers between devices, shared(): lax.all_to_all(spread_rows, axis, 0, 0, tiled=True)  18 us
    dot_general x4, matrix products, outer_sum(): lax.dot_general(former, latter, (((0,), (0,)), ((), ())), preferred_eleme...  12.4 us
  transfers between devices with their start and end apart: 18, of which 12 were waited for; matrix products, arithmetic and copies ran while one was open for 15% of the time, Pallas kernels for 0%

profile of v2, /device:TPU:0, one launch (start us, length us, event | category | flops | bytes accessed | tf_op | source)
XLA Modules:
  0.0 499.4 jit_solution(6413147844436742400)
XLA Ops:
  10.1 12.2 %all_to_all.118 = bf16[4,32,1792]{2,1,0:T(8,128)(2,1)S(1)} all-to-all(bf16[4,32,1792]{2,1,0:T(8,128)(2,1)S(1)} %pad_maximum_fusion.1), channel_id=1, replica_groups=mesh['dp'=8,'ctx'=4] {'ctx'}, dimensions={0} | all-to-all | bytes 917504 | tf_op jit(solution)/shard_map/all_to_all | solution.py:115
  24.8 12.0 %all_to_all.119 = bf16[32,2,192]{2,1,0:T(2,128)(2,1)S(1)} all-to-all(bf16[32,2,192]{2,1,0:T(2,128)(2,1)S(1)} %reshape.584), channel_id=1, replica_groups=mesh['dp'=8,'ctx'=4] {'dp','ctx'}, dimensions={0} | all-to-all | bytes 49152 | tf_op jit(solution)/shard_map/all_to_all | solution.py:52
  37.9 3.5 all-to-all-start
  44.0 11.8 %all-to-all-done = bf16[4,128,1024]{2,1,0:T(8,128)(2,1)S(1)} async-done(((bf16[4,128,1024]{2,1,0:T(8,128)(2,1)}), bf16[4,128,1024]{2,1,0:T(8,128)(2,1)S(1)}, u32[]{:S(2)}, u32[]{:S(2)}) %all-to-all-start) | async-done | bytes 1048608 | tf_op jit(solution)/shard_map/all_to_all | solution.py:52
  57.0 3.6 all-to-all-start.3
  60.9 67.3 %all_gather.9 = bf16[256,1024]{1,0:T(8,128)(2,1)S(1)} all-gather(bf16[32,1024]{1,0:T(8,128)(2,1)S(1)} %copy-done.18), channel_id=1, replica_groups=mesh['dp'=8,'ctx'=4] {'dp'}, dimensions={0}, use_global_device_ids=true | all-gather | bytes 589824 | tf_op jit(solution)/shard_map/all_gather | solution.py:121
  135.8 1.8 broadcast_in_dim.49
  137.6 3.6 all-to-all-start.5
  145.2 1.8 copy.76
  147.0 1.8 copy.77
  148.8 1.8 copy.75
  150.6 2.5 fusion
  153.1 1.9 copy-done.28
  160.0 6.8 %all-to-all-done.5 = bf16[4,256,1024]{2,1,0:T(8,128)(2,1)S(1)} async-done(((bf16[4,256,1024]{2,1,0:T(8,128)(2,1)}), bf16[4,256,1024]{2,1,0:T(8,128)(2,1)S(1)}, u32[]{:S(2)}, u32[]{:S(2)}) %all-to-all-start.5) | async-done | bytes 2097184 | tf_op jit(solution)/shard_map/all_to_all | solution.py:52
  166.8 4.1 all-to-all-start.4
  172.6 4.3 all-to-all-done.4
  176.9 2.2 fusion.68
  179.7 17.6 %all_to_all.120 = bf16[4,128,1024]{2,1,0:T(8,128)(2,1)} all-to-all(bf16[4,128,1024]{2,1,0:T(8,128)(2,1)S(1)} %broadcast_in_dim.50), channel_id=1, replica_groups=mesh['dp'=8,'ctx'=4] {'ctx'}, dimensions={0} | all-to-all | bytes 2097152 | tf_op jit(solution)/shard_map/all_to_all | solution.py:52
  198.4 3.7 all-to-all-start.8
  202.8 4.5 fusion.71
  207.3 9.0 %all-to-all-done.8 = bf16[4,128,1024]{2,1,0:T(8,128)(2,1)S(1)} async-done(((bf16[4,128,1024]{2,1,0:T(8,128)(2,1)}), bf16[4,128,1024]{2,1,0:T(8,128)(2,1)S(1)}, u32[]{:S(2)}, u32[]{:S(2)}) %all-to-all-start.8) | async-done | bytes 1048608 | tf_op jit(solution)/shard_map/all_to_all | solution.py:52
  216.3 5.1 %fusion.69 = (f32[1024]{0:T(1024)S(1)}, bf16[512,1024]{1,0:T(8,128)(2,1)S(1)}) fusion(f32[512,1024]{1,0:T(8,128)} %fusion.71, f32[1024]{0:T(1024)S(1)} %bitcast.171, bf16[512,1024]{1,0:T(8,128)(2,1)S(1)} %bitcast.146, bf16[1024,1024]{1,0:T(8,128)(2,1)} %all-gather.5.cloned.1.call-done), kind=kOutput, calls=%fused_computation.144 | convolution fusion | flops 1084750848 | bytes 6299648 | tf_op jit(solution)/shard_map/dot_general | solution.py:45
  221.4 2.3 convolution_convert_fusion.4
  223.7 3.5 all-to-all-start.9
  227.3 4.8 convolution_convert_fusion.5
  232.1 9.5 %all-to-all-done.9 = bf16[4,128,1024]{2,1,0:T(8,128)(2,1)S(1)} async-done(((bf16[4,128,1024]{2,1,0:T(8,128)(2,1)}), bf16[4,128,1024]{2,1,0:T(8,128)(2,1)S(1)}, u32[]{:S(2)}, u32[]{:S(2)}) %all-to-all-start.9) | async-done | bytes 1048608 | tf_op jit(solution)/shard_map/all_to_all | solution.py:56
  242.6 4.2 all-to-all-start.7
  246.9 1.7 convert_reduce_fusion.2
  248.9 12.5 %all-to-all-done.7 = bf16[4,128,1024]{2,1,0:T(8,128)(2,1)} async-done(((bf16[4,128,1024]{2,1,0:T(8,128)(2,1)}), bf16[4,128,1024]{2,1,0:T(8,128)(2,1)}, u32[]{:S(2)}, u32[]{:S(2)}) %all-to-all-start.7) | async-done | bytes 1048608 | tf_op jit(solution)/shard_map/all_to_all | solution.py:56
  265.1 3.6 all-to-all-start.10
  268.7 14.4 %all-to-all-done.10 = bf16[4,128,1024]{2,1,0:T(8,128)(2,1)S(1)} async-done(((bf16[4,128,1024]{2,1,0:T(8,128)(2,1)}), bf16[4,128,1024]{2,1,0:T(8,128)(2,1)S(1)}, u32[]{:S(2)}, u32[]{:S(2)}) %all-to-all-start.10) | async-done | bytes 1048608 | tf_op jit(solution)/shard_map/all_to_all | solution.py:52
  284.7 3.7 multiply_convert_fusion
  292.4 2.0 convolution_convert_fusion.3
  294.4 4.5 all-to-all-start.11
  298.9 4.2 convolution_convert_fusion.1
  303.0 10.1 %all-to-all-done.11 = bf16[4,128,1024]{2,1,0:T(8,128)(2,1)} async-done(((bf16[4,128,1024]{2,1,0:T(8,128)(2,1)}), bf16[4,128,1024]{2,1,0:T(8,128)(2,1)}, u32[]{:S(2)}, u32[]{:S(2)}) %all-to-all-start.11) | async-done | bytes 1048608 | tf_op jit(solution)/shard_map/all_to_all | solution.py:56
  313.1 5.8 %all-to-all-start.13 = ((bf16[8,128,1024]{2,1,0:T(8,128)(2,1)}), bf16[8,128,1024]{2,1,0:T(8,128)(2,1)}, u32[]{:S(2)}, u32[]{:S(2)}) async-start(bf16[8,128,1024]{2,1,0:T(8,128)(2,1)} %bitcast.132), calls=%async_computation.13 | async-start | bytes 4194304 | tf_op jit(solution)/shard_map/all_to_all | solution.py:56
  320.3 4.8 convolution_convert_fusion
  326.1 2.2 convolution_convert_fusion.2
  328.4 42.9 %all-to-all-done.13 = bf16[8,128,1024]{2,1,0:T(8,128)(2,1)} async-done(((bf16[8,128,1024]{2,1,0:T(8,128)(2,1)}), bf16[8,128,1024]{2,1,0:T(8,128)(2,1)}, u32[]{:S(2)}, u32[]{:S(2)}) %all-to-all-start.13) | async-done | bytes 2097184 | tf_op jit(solution)/shard_map/all_to_all | solution.py:56
  371.2 3.6 all-to-all-start.12
  381.0 2.0 reduce_sum.267
  383.0 31.2 %all-to-all-done.12 = bf16[8,128,768]{2,1,0:T(8,128)(2,1)S(1)} async-done(((bf16[8,128,768]{2,1,0:T(8,128)(2,1)}), bf16[8,128,768]{2,1,0:T(8,128)(2,1)S(1)}, u32[]{:S(2)}, u32[]{:S(2)}) %all-to-all-start.12) | async-done | bytes 1572896 | tf_op jit(solution)/shard_map/all_to_all | solution.py:56
  414.2 2.7 all-to-all-start.15
  417.9 6.3 %all-to-all-done.15 = f32[32,1,384]{2,1,0:T(1,128)S(1)} async-done(((f32[32,1,384]{2,1,0:T(1,128)}), f32[32,1,384]{2,1,0:T(1,128)S(1)}, u32[]{:S(2)}, u32[]{:S(2)}) %all-to-all-start.15) | async-done | bytes 49184 | tf_op jit(solution)/shard_map/all_to_all | solution.py:56
  424.2 3.5 all-to-all-start.14
  433.5 54.6 %reduce-scatter.5.cloned.1.call-done = bf16[128,1024]{1,0:T(8,128)(2,1)} async-done(((bf16[1024,1024]{1,0:T(8,128)(2,1)}), bf16[128,1024]{1,0:T(8,128)(2,1)}) %reduce-scatter.5.cloned.1.call-update) | async-done | bytes 262160 | tf_op jit(solution)/shard_map/reduce_scatter | solution.py:235
  488.1 1.8 convert_element_type.154
  (211 shorter events, 59.8 us)
Async XLA Ops:
  7.2 195.7 %all-gather.3.cloned.1.call-start = ((), (), s32[]{:S(2)}) async-start(), calls=%async_computation.18 | async-start | bytes 2359296 | tf_op jit(solution)/shard_map/all_gather | solution.py:128
  8.5 14.5 %copy-start.23 = (bf16[2,32]{1,0:T(2,128)(2,1)S(1)}, bf16[2,32]{1,0:T(2,128)(2,1)}, u32[]{:S(2)}) copy-start(bf16[2,32]{1,0:T(2,128)(2,1)} %param.20) | copy-start | bytes 388
  8.5 14.6 %copy-start.24 = (bf16[2,32]{1,0:T(2,128)(2,1)S(1)}, bf16[2,32]{1,0:T(2,128)(2,1)}, u32[]{:S(2)}) copy-start(bf16[2,32]{1,0:T(2,128)(2,1)} %param.21) | copy-start | bytes 388
  8.5 14.6 %copy-start.22 = (bf16[4,32]{1,0:T(4,128)(2,1)S(1)}, bf16[4,32]{1,0:T(4,128)(2,1)}, u32[]{:S(2)}) copy-start(bf16[4,32]{1,0:T(4,128)(2,1)} %param.22) | copy-start | bytes 772
  8.5 14.7 %copy-start.20 = (bf16[128]{0:T(256)(128)(2,1)S(1)}, bf16[128]{0:T(256)(128)(2,1)}, u32[]{:S(2)}) copy-start(bf16[128]{0:T(256)(128)(2,1)} %param.23) | copy-start | bytes 772
  8.6 28.2 %copy-start = (bf16[128,1024]{1,0:T(8,128)(2,1)S(1)}, bf16[128,1024]{1,0:T(8,128)(2,1)}, u32[]{:S(2)}) copy-start(bf16[128,1024]{1,0:T(8,128)(2,1)} %param.12) | copy-start | bytes 786436
  23.0 19.7 %copy-start.19 = (s32[1,512]{1,0:T(1,128)S(1)}, s32[1,512]{1,0:T(1,128)}, u32[]{:S(2)}) copy-start(s32[1,512]{1,0:T(1,128)} %param.14) | copy-start | bytes 6148
  23.0 20.4 %copy-start.25 = (s32[1,8]{1,0:T(1,128)S(1)}, s32[1,8]{1,0:T(1,128)}, u32[]{:S(2)}) copy-start(s32[1,8]{1,0:T(1,128)} %param.15) | copy-start | bytes 100
  37.9 17.9 %all-to-all-start = ((bf16[4,128,1024]{2,1,0:T(8,128)(2,1)}), bf16[4,128,1024]{2,1,0:T(8,128)(2,1)S(1)}, u32[]{:S(2)}, u32[]{:S(2)}) async-start(bf16[4,128,1024]{2,1,0:T(8,128)(2,1)} %broadcast_in_dim.42), calls=%async_computation | async-start | bytes 2097152 | tf_op jit(solution)/shard_map/all_to_all | solution.py:52
  41.4 174.9 %all-gather.5.cloned.1.call-start = ((), (), s32[]{:S(2)}) async-start(), calls=%async_computation.19 | async-start | bytes 2359296 | tf_op jit(solution)/shard_map/all_gather | solution.py:129
  44.0 17.0 %copy-start.18 = (bf16[32,1024]{1,0:T(8,128)(2,1)S(1)}, bf16[32,1024]{1,0:T(8,128)(2,1)}, u32[]{:S(2)}) copy-start(bf16[32,1024]{1,0:T(8,128)(2,1)} %param.17) | copy-start | bytes 196612
  57.0 78.7 %all-to-all-start.3 = ((bf16[8,128,768]{2,1,0:T(8,128)(2,1)}), bf16[8,128,768]{2,1,0:T(8,128)(2,1)S(1)}, u32[]{:S(2)}, u32[]{:S(2)}) async-start(bf16[8,128,768]{2,1,0:T(8,128)(2,1)} %broadcast_in_dim.44), calls=%async_computation.3 | async-start | bytes 3145728 | tf_op jit(solution)/shard_map/all_to_all | solution.py:52
  135.7 1.8 copy-start.2
  137.6 29.2 %all-to-all-start.5 = ((bf16[4,256,1024]{2,1,0:T(8,128)(2,1)}), bf16[4,256,1024]{2,1,0:T(8,128)(2,1)S(1)}, u32[]{:S(2)}, u32[]{:S(2)}) async-start(bf16[4,256,1024]{2,1,0:T(8,128)(2,1)} %broadcast_in_dim.49), calls=%async_computation.5 | async-start | bytes 4194304 | tf_op jit(solution)/shard_map/all_to_all | solution.py:52
  141.2 1.4 copy-start.3
  150.6 4.4 copy-start.13
  150.6 4.4 copy-start.16
  153.0 1.9 copy-start.28
  166.8 10.1 %all-to-all-start.4 = ((bf16[4,128,256]{1,2,0:T(8,128)(2,1)}), bf16[4,128,256]{1,2,0:T(8,128)(2,1)}, u32[]{:S(2)}, u32[]{:S(2)}) async-start(bf16[4,128,256]{1,2,0:T(8,128)(2,1)} %copy.79), calls=%async_computation.4 | async-start | bytes 524288 | tf_op jit(solution)/shard_map/all_to_all | solution.py:167
  179.4 17.9 %copy-start.5 = (bf16[128,1024]{1,0:T(8,128)(2,1)S(1)}, bf16[128,1024]{1,0:T(8,128)(2,1)}, u32[]{:S(2)}) copy-start(bf16[128,1024]{1,0:T(8,128)(2,1)} %param.13) | copy-start | bytes 786436
  198.4 17.9 %all-to-all-start.8 = ((bf16[4,128,1024]{2,1,0:T(8,128)(2,1)}), bf16[4,128,1024]{2,1,0:T(8,128)(2,1)S(1)}, u32[]{:S(2)}, u32[]{:S(2)}) async-start(bf16[4,128,1024]{2,1,0:T(8,128)(2,1)} %broadcast_in_dim.51), calls=%async_computation.8 | async-start | bytes 2097152 | tf_op jit(solution)/shard_map/all_to_all | solution.py:52
  216.3 5.1 %copy-start.10 = (bf16[4,128,1024]{2,1,0:T(8,128)(2,1)}, bf16[4,128,1024]{2,1,0:T(8,128)(2,1)S(1)}, u32[]{:S(2)}) copy-start(bf16[4,128,1024]{2,1,0:T(8,128)(2,1)S(1)} %all-to-all-done.8) | copy-start | bytes 3145732
  216.3 5.1 %copy-start.21 = (bf16[1024,1024]{1,0:T(8,128)(2,1)S(1)}, bf16[1024,1024]{1,0:T(8,128)(2,1)}, u32[]{:S(2)}) copy-start(bf16[1024,1024]{1,0:T(8,128)(2,1)} %all-gather.3.cloned.1.call-done) | copy-start | bytes 6291460
  221.4 2.3 copy-start.30
  223.7 17.9 %all-to-all-start.9 = ((bf16[4,128,1024]{2,1,0:T(8,128)(2,1)}), bf16[4,128,1024]{2,1,0:T(8,128)(2,1)S(1)}, u32[]{:S(2)}, u32[]{:S(2)}) async-start(bf16[4,128,1024]{2,1,0:T(8,128)(2,1)} %bitcast.151), calls=%async_computation.9 | async-start | bytes 2097152 | tf_op jit(solution)/shard_map/all_to_all | solution.py:56
  241.6 1.0 copy-start.1
  242.6 18.7 %all-to-all-start.7 = ((bf16[4,128,1024]{2,1,0:T(8,128)(2,1)}), bf16[4,128,1024]{2,1,0:T(8,128)(2,1)}, u32[]{:S(2)}, u32[]{:S(2)}) async-start(bf16[4,128,1024]{2,1,0:T(8,128)(2,1)} %bitcast.150), calls=%async_computation.7 | async-start | bytes 2097152 | tf_op jit(solution)/shard_map/all_to_all | solution.py:56
  246.9 16.0 %copy-start.6 = (bf16[128,1024]{1,0:T(8,128)(2,1)S(1)}, bf16[128,1024]{1,0:T(8,128)(2,1)}, u32[]{:S(2)}) copy-start(bf16[128,1024]{1,0:T(8,128)(2,1)} %param.13) | copy-start | bytes 786436
  263.9 19.2 %copy-start.7 = (bf16[512,4,64]{0,2,1:T(8,128)(2,1)S(1)}, bf16[512,4,64]{0,2,1:T(8,128)(2,1)}, u32[]{:S(2)}) copy-start(bf16[512,4,64]{0,2,1:T(8,128)(2,1)} %fusion.34) | copy-start | bytes 786436
  265.1 19.6 %copy-start.14 = (pred[512,512]{0,1:T(8,128)(4,1)S(1)}, pred[512,512]{0,1:T(8,128)(4,1)}, u32[]{:S(2)}) copy-start(pred[512,512]{0,1:T(8,128)(4,1)} %compare_and_fusion) | copy-start | bytes 786436
  265.1 18.1 %all-to-all-start.10 = ((bf16[4,128,1024]{2,1,0:T(8,128)(2,1)}), bf16[4,128,1024]{2,1,0:T(8,128)(2,1)S(1)}, u32[]{:S(2)}, u32[]{:S(2)}) async-start(bf16[4,128,1024]{2,1,0:T(8,128)(2,1)} %broadcast_in_dim.52), calls=%async_computation.10 | async-start | bytes 2097152 | tf_op jit(solution)/shard_map/all_to_all | solution.py:52
  283.1 1.6 copy-start.17
  284.7 3.8 copy-start.9
  288.5 1.0 copy-start.8
  288.5 1.7 copy-start.15
  288.5 2.3 copy-start.29
  290.9 1.1 copy-start.11
  290.9 1.5 copy-start.4
  292.0 2.4 copy-start.26
  294.4 18.8 %all-to-all-start.11 = ((bf16[4,128,1024]{2,1,0:T(8,128)(2,1)}), bf16[4,128,1024]{2,1,0:T(8,128)(2,1)}, u32[]{:S(2)}, u32[]{:S(2)}) async-start(bf16[4,128,1024]{2,1,0:T(8,128)(2,1)} %bitcast.152), calls=%async_computation.11 | async-start | bytes 2097152 | tf_op jit(solution)/shard_map/all_to_all | solution.py:56
  313.1 58.1 %all-to-all-start.13 = ((bf16[8,128,1024]{2,1,0:T(8,128)(2,1)}), bf16[8,128,1024]{2,1,0:T(8,128)(2,1)}, u32[]{:S(2)}, u32[]{:S(2)}) async-start(bf16[8,128,1024]{2,1,0:T(8,128)(2,1)} %bitcast.132), calls=%async_computation.13 | async-start | bytes 4194304 | tf_op jit(solution)/shard_map/all_to_all | solution.py:56
  319.0 111.0 %reduce-scatter.3.cloned.1.call-start = ((), (), s32[]{:S(2)}) async-start(), calls=%async_computation.20 | async-start | bytes 589824 | tf_op jit(solution)/shard_map/reduce_scatter | solution.py:235
  320.3 167.8 %reduce-scatter.5.cloned.1.call-start = ((), (), s32[]{:S(2)}) async-start(), calls=%async_computation.21 | async-start | bytes 2359296 | tf_op jit(solution)/shard_map/reduce_scatter | solution.py:235
  325.1 1.0 copy-start.27
  371.2 42.9 %all-to-all-start.12 = ((bf16[8,128,768]{2,1,0:T(8,128)(2,1)}), bf16[8,128,768]{2,1,0:T(8,128)(2,1)S(1)}, u32[]{:S(2)}, u32[]{:S(2)}) async-start(bf16[8,128,768]{2,1,0:T(8,128)(2,1)} %bitcast.139), calls=%async_computation.12 | async-start | bytes 3145728 | tf_op jit(solution)/shard_map/all_to_all | solution.py:56
  414.2 10.1 %all-to-all-start.15 = ((f32[32,1,384]{2,1,0:T(1,128)}), f32[32,1,384]{2,1,0:T(1,128)S(1)}, u32[]{:S(2)}, u32[]{:S(2)}) async-start(f32[32,1,384]{2,1,0:T(1,128)} %copy.87), calls=%async_computation.17 | async-start | bytes 98304 | tf_op jit(solution)/shard_map/all_to_all | solution.py:56
  424.2 65.7 %all-to-all-start.14 = ((bf16[4,32,1792]{2,1,0:T(8,128)(2,1)}), bf16[4,32,1792]{2,1,0:T(8,128)(2,1)S(1)}, u32[]{:S(2)}, u32[]{:S(2)}) async-start(bf16[4,32,1792]{2,1,0:T(8,128)(2,1)} %bitcast.42), calls=%async_computation.14 | async-start | bytes 917504 | tf_op jit(solution)/shard_map/all_to_all | solution.py:256
  430.0 2.9 collective-permute-start
  (1 other events, 0.9 us)
Sparse Core Ops, SparseCore 0:
  23.1 58.7 all-gather.2
  84.0 61.2 all-gather.4
  323.7 91.8 reduce-scatter.2
  419.0 69.0 reduce-scatter.4
